TPU v7x, 32 devices: a whole 2x2x4 slice. The times are simulated.
32 devices in a mesh: rcv: 8 (over z, y), src: 4 (over x, core).
Axes of the slice: x: 2, y: 2, z: 4, core: 2. Of those that a mesh axis runs over, the one named last changes fastest.
Arguments:
- k_op: bfloat16 [2, 3072, 3072], P(None, 'rcv', 'src'), may hold values from -0.078125 to 0.078125
- data: bfloat16 [2, 3072, 3072], P(None, 'rcv', 'src'), may hold values from -6 to 6
- factor: bfloat16 [2, 4, 768, 128], P(None, 'src', 'rcv'), may hold values from -1.796875 to 1.796875
Outputs:
- gradient: float32 [2, 4, 768, 128], P(None, 'src', 'rcv')
All inputs are finite; a program needn't handle non-finite values.
Results may differ from a plain program's by a relative error of at most 0.0019.
Values may be sent and summed in bfloat16 or wider, within the bound.
A program may use at most 64 MiB of HBM per device.

v0:
```python
import math
import jax
import jax.numpy as jnp
from jax import lax
from jax.sharding import PartitionSpec as P


def plain_dot(left, right):
    return jnp.dot(left, right, preferred_element_type=jnp.float32)


def contract_last(left, right):
    return lax.dot_general(
        left, right, (((1,), (1,)), ((), ())), preferred_element_type=jnp.float32
    )


def contract_first(left, right):
    return lax.dot_general(
        left, right, (((0,), (0,)), ((), ())), preferred_element_type=jnp.float32
    )


def body(k_op, data, factor):
    row_count = k_op.shape[1]
    receivers = row_count * lax.axis_size("rcv")
    gathered = lax.all_gather(factor, "rcv", axis=2, tiled=True)
    factor_real = gathered[0, 0]
    factor_imaginary = gathered[1, 0]
    kernel_real = k_op[0]
    kernel_imaginary = k_op[1]
    modeled_part = jnp.stack(
        [
            plain_dot(kernel_real, factor_real) - plain_dot(kernel_imaginary, factor_imaginary),
            plain_dot(kernel_real, factor_imaginary) + plain_dot(kernel_imaginary, factor_real),
        ]
    )
    modeled = lax.psum(modeled_part, "src").astype(jnp.bfloat16)
    modeled_real = modeled[0]
    modeled_imaginary = modeled[1]
    error_real = (
        contract_last(modeled_real, factor_real)
        - contract_last(modeled_imaginary, factor_imaginary)
        - data[0].astype(jnp.float32)
    ).astype(jnp.bfloat16)
    error_imaginary = (
        contract_last(modeled_real, factor_imaginary)
        + contract_last(modeled_imaginary, factor_real)
        - data[1].astype(jnp.float32)
    ).astype(jnp.bfloat16)
    weighted_part = jnp.stack(
        [
            plain_dot(error_real, factor_real) + plain_dot(error_imaginary, factor_imaginary),
            plain_dot(error_imaginary, factor_real) - plain_dot(error_real, factor_imaginary),
        ]
    )
    mirror = jnp.stack(
        [
            contract_first(error_real, modeled_real)
            + contract_first(error_imaginary, modeled_imaginary),
            contract_first(error_imaginary, modeled_real)
            - contract_first(error_real, modeled_imaginary),
        ]
    )
    weighted = lax.psum(weighted_part, "src").astype(jnp.bfloat16)
    weighted_real = weighted[0]
    weighted_imaginary = weighted[1]
    projected = jnp.stack(
        [
            contract_first(kernel_real, weighted_real)
            + contract_first(kernel_imaginary, weighted_imaginary),
            contract_first(kernel_real, weighted_imaginary)
            - contract_first(kernel_imaginary, weighted_real),
        ]
    )
    summed = lax.psum_scatter(projected + mirror, "rcv", scatter_dimension=1, tiled=True)
    scaling = 1.0 / math.sqrt(receivers)
    return (summed * scaling)[:, None]


def solution(mesh):
    return jax.shard_map(
        body,
        mesh=mesh,
        in_specs=(P(None, "rcv", "src"), P(None, "rcv", "src"), P(None, "src", "rcv", None)),
        out_specs=P(None, "src", "rcv", None),
        check_vma=False,
    )
```

profile of v0, /device:TPU:0, one launch (start us, length us, event | category | flops | bytes accessed | tf_op | source)
XLA Modules:
  0.0 163.0 jit_solution(13344070304495948577)
XLA Ops:
  6.5 33.1 %all_gather.3 = bf16[2,1,768,128]{3,2,1,0:T(8,128)(2,1)S(1)} all-gather(bf16[2,1,96,128]{3,2,1,0:T(8,128)(2,1)} %param.5), channel_id=1, replica_groups=mesh['rcv'=8,'src'=4] {'rcv'}, dimensions={2}, use_global_device_ids=true | all-gather | bytes 442368 | tf_op jit(solution)/shard_map/all_gather | solution.py:27
  39.6 1.4 fusion.20
  41.0 0.3 fusion.22
  41.4 0.3 fusion.10
  41.7 0.3 fusion.11
  42.0 14.5 %all-reduce.6 = bf16[2,384,128]{2,1,0:T(8,128)(2,1)S(1)} all-reduce(f32[2,384,128]{2,1,0:T(8,128)S(1)} %pad_maximum_fusion), channel_id=1, replica_groups=mesh['rcv'=8,'src'=4] {'src'}, use_global_device_ids=true, to_apply=%region_0.0 | all-reduce | flops 98304 | bytes 589824 | tf_op jit(solution)/shard_map/psum | solution.py:38
  56.6 0.3 fusion.36
  56.9 0.3 fusion.35
  57.2 0.6 copy-done.1
  58.2 0.3 fusion.33
  58.5 0.3 fusion.2
  58.8 0.3 fusion.34
  59.1 0.3 fusion.8
  59.5 0.3 fusion.9
  59.8 14.4 %all-reduce.7 = bf16[2,384,128]{2,1,0:T(8,128)(2,1)S(1)} all-reduce(f32[2,384,128]{2,1,0:T(8,128)S(1)} %pad_maximum_fusion.1), channel_id=1, replica_groups=mesh['rcv'=8,'src'=4] {'src'}, use_global_device_ids=true, to_apply=%region_1.0 | all-reduce | flops 98304 | bytes 589824 | tf_op jit(solution)/shard_map/psum | solution.py:65
  74.8 0.3 fusion.37
  75.2 0.3 fusion.38
  76.1 0.3 fusion.4
  76.4 0.3 fusion.5
  76.8 1.2 copy.13
  78.0 0.6 dynamic-slice
  79.3 75.3 %all-reduce.5.cloned.1.call-done = f32[2,768,128]{2,0,1:T(2,128)} async-done(((f32[2,768,128]{2,0,1:T(2,128)}), f32[2,768,128]{2,0,1:T(2,128)}) %all-reduce.5.cloned.1.call-update) | async-done | bytes 786448
  154.5 0.9 fusion.32
  155.5 0.6 copy.14
  (15 shorter events, 1.6 us)
Async XLA Ops:
  6.5 34.5 %copy-start = (bf16[2,384,768]{2,1,0:T(8,128)(2,1)S(1)}, bf16[2,384,768]{2,1,0:T(8,128)(2,1)}, u32[]{:S(2)}) copy-start(bf16[2,384,768]{2,1,0:T(8,128)(2,1)} %param.3) | copy-start | bytes 3538948
  6.5 148.0 %all-reduce.5.cloned.1.call-start = ((), (), s32[]{:S(2)}) async-start(), calls=%async_computation | async-start | bytes 1572864
  56.6 1.3 copy-start.1
  76.8 1.2 copy-start.2
Sparse Core Ops, SparseCore 0:
  78.1 76.3 all-reduce.4
where the time goes:
time: 163 us
  waiting for transfers between devices  75.3 us (46%)
  blocking collectives  62.1 us (38%)
  between operations  14.2 us (9%)
  matrix products  7.23 us (4%)
  local copies, waits for them, and re-layouts  3.06 us (2%)
    unnamed x2, waiting for transfers between devices  75.3 us
    all_gather x1, blocking collectives, body(): gathered = lax.all_gather(factor, 'rcv', axis=2, tiled=True)  33.1 us
    psum x1, blocking collectives, body(): modeled = lax.psum(modeled_part, 'src').astype(jnp.bfloat16)  14.5 us
    psum x1, blocking collectives, body(): weighted = lax.psum(weighted_part, 'src').astype(jnp.bfloat16)  14.4 us
    dot_general x8, matrix products, plain_dot(): return jnp.dot(left, right, preferred_element_type=jnp.float32)  3.58 us
  transfers between devices with their start and end apart: 1, of which 1 were waited for; matrix products, arithmetic and copies ran while one was open for 0% of the time, Pallas kernels for 0%

commit v1 on v0

--- a/solution.py
+++ b/solution.py
@@ -35,7 +35,7 @@
             plain_dot(kernel_real, factor_imaginary) + plain_dot(kernel_imaginary, factor_real),
         ]
     )
-    modeled = lax.psum(modeled_part, "src").astype(jnp.bfloat16)
+    modeled = jnp.sum(lax.all_gather(modeled_part, "src"), axis=0).astype(jnp.bfloat16)
     modeled_real = modeled[0]
     modeled_imaginary = modeled[1]
     error_real = (

time: 163 us -> 172 us (1.055)
  waiting for transfers between devices: 75.3 us -> 95.6 us
  blocking collectives: 62.1 us -> 48 us
  other arithmetic: 1.09 us -> 3.33 us
    all_gather x0 -> x1, waiting for transfers between devices: none -> 20.8 us  [body(): lax.all_gather(modeled_part, 'src')]
    psum x1 -> x0, blocking collectives: 14.5 us -> none  [body(): modeled = lax.psum(modeled_part, 'src').astype(jnp.bfloat16)]
    unnamed x2 -> x3, waiting for transfers between devices: 75.3 us -> 74.8 us
  transfers between devices with their start and end apart: 1 -> 2, of which waited for: 1 -> 2; matrix products, arithmetic and copies ran while one was open for 0% -> 0% of each run, Pallas kernels for 0% -> 0%
where the time goes in v1:
time: 172 us
  waiting for transfers between devices  95.6 us (56%)
  blocking collectives  48 us (28%)
  between operations  14.2 us (8%)
  matrix products  7.23 us (4%)
  other arithmetic  3.33 us (2%)
  local copies, waits for them, and re-layouts  3.07 us (2%)
    unnamed x3, waiting for transfers between devices  74.8 us
    all_gather x1, blocking collectives, body(): gathered = lax.all_gather(factor, 'rcv', axis=2, tiled=True)  33.1 us
    all_gather x1, waiting for transfers between devices, body(): lax.all_gather(modeled_part, 'src')  20.8 us
    psum x1, blocking collectives, body(): weighted = lax.psum(weighted_part, 'src').astype(jnp.bfloat16)  14.9 us
    dot_general x8, matrix products, plain_dot(): return jnp.dot(left, right, preferred_element_type=jnp.float32)  3.6 us
  transfers between devices with their start and end apart: 2, of which 2 were waited for; matrix products, arithmetic and copies ran while one was open for 0% of the time, Pallas kernels for 0%

profile of v1, /device:TPU:0, one launch (start us, length us, event | category | flops | bytes accessed | tf_op | source)
XLA Modules:
  0.0 171.5 jit_solution(4635274211374891299)
XLA Ops:
  6.5 33.1 %all_gather.9 = bf16[2,1,768,128]{3,2,1,0:T(8,128)(2,1)S(1)} all-gather(bf16[2,1,96,128]{3,2,1,0:T(8,128)(2,1)} %param.5), channel_id=1, replica_groups=mesh['rcv'=8,'src'=4] {'rcv'}, dimensions={2}, use_global_device_ids=true | all-gather | bytes 442368 | tf_op jit(solution)/shard_map/all_gather | solution.py:27
  39.6 1.4 fusion.20
  41.0 0.3 fusion.22
  41.4 0.3 fusion.10
  41.7 0.3 fusion.11
  42.0 0.8 pad_maximum_fusion
  42.8 20.8 %all-gather.3.cloned.1.call-done = f32[8,384,128]{2,1,0:T(8,128)} async-done(((f32[2,384,128]{2,1,0:T(8,128)}), f32[8,384,128]{2,1,0:T(8,128)}) %all-gather.3.cloned.1.call-update) | async-done | bytes 1572880 | tf_op jit(solution)/shard_map/all_gather | solution.py:38
  63.6 1.5 reduce_sum.9
  65.8 0.6 copy-done.1
  66.4 0.3 fusion.3
  66.8 0.3 fusion.33
  67.1 0.3 fusion.2
  67.4 0.3 fusion.34
  67.7 0.3 fusion.8
  68.0 0.3 fusion.9
  68.4 14.9 %all-reduce.5 = bf16[2,384,128]{2,1,0:T(8,128)(2,1)S(1)} all-reduce(f32[2,384,128]{2,1,0:T(8,128)S(1)} %pad_maximum_fusion.1), channel_id=1, replica_groups=mesh['rcv'=8,'src'=4] {'src'}, use_global_device_ids=true, to_apply=%region_1.0 | all-reduce | flops 98304 | bytes 589824 | tf_op jit(solution)/shard_map/psum | solution.py:65
  83.9 0.3 fusion.37
  85.1 0.3 fusion.4
  85.5 0.3 fusion.5
  85.9 1.2 copy.13
  87.1 0.6 dynamic-slice
  88.3 74.8 %all-reduce.4.cloned.1.call-done = f32[2,768,128]{2,0,1:T(2,128)} async-done(((f32[2,768,128]{2,0,1:T(2,128)}), f32[2,768,128]{2,0,1:T(2,128)}) %all-reduce.4.cloned.1.call-update) | async-done | bytes 786448
  163.1 0.9 fusion.32
  164.0 0.6 copy.14
  (18 shorter events, 2.3 us)
Async XLA Ops:
  6.5 34.5 %copy-start = (bf16[2,384,768]{2,1,0:T(8,128)(2,1)S(1)}, bf16[2,384,768]{2,1,0:T(8,128)(2,1)}, u32[]{:S(2)}) copy-start(bf16[2,384,768]{2,1,0:T(8,128)(2,1)} %param.3) | copy-start | bytes 3538948
  6.5 57.1 %all-gather.3.cloned.1.call-start = ((), (), s32[]{:S(2)}) async-start(), calls=%async_computation | async-start | bytes 1966080 | tf_op jit(solution)/shard_map/all_gather | solution.py:38
  42.8 120.3 %all-reduce.4.cloned.1.call-start = ((), (), s32[]{:S(2)}) async-start(), calls=%async_computation.1 | async-start | bytes 1572864
  65.2 1.3 copy-start.1
  85.9 1.2 copy-start.2
Sparse Core Ops, SparseCore 0:
  42.9 20.6 all-gather.2
  87.2 75.8 all-reduce.3
